TPU v7x, 512 devices: a whole 4x4x16 slice. The times are simulated.
512 devices in a mesh: blk: 128 (over y_hi, z, x), feat: 4 (over y_lo, core).
Axes of the slice: x: 4, y: 4 (y_hi: 2, y_lo: 2; y = y_hi * 2 + y_lo), z: 16, core: 2. Of those that a mesh axis runs over, the one named last changes fastest.
Arguments:
- features: bfloat16 [256, 131072], P('feat', 'blk'), may hold values from -6 to 6
- block_values: bfloat16 [17408, 128, 128], P('blk'), may hold values from 0 to 1, as said below
- block_rows: int32 [17408], P('blk'), may hold values from 0 to 7, as said below
- block_cols: int32 [17408], P('blk'), may hold values from 0 to 1023, as said below
- block_count: int32 [128], P('blk'), may hold values from 8 to 136, as said below
- labels: int32 [131072], P(('blk', 'feat')), may hold values from 0 to 127
- weight_in: bfloat16 [256, 256], replicated, may hold values from -0.375 to 0.375
- weight_out: bfloat16 [256, 128], replicated, may hold values from -1 to 1
Outputs:
- logits: float32 [128, 131072], P(None, ('blk', 'feat'))
- grad_in: float32 [256, 256], replicated
- grad_out: float32 [256, 128], replicated
Inputs may be any that keep to these rules, and one draw needn't show every extreme that they name: The first block_count[s] slots of stripe s are its blocks; the remaining slots hold blocks that are not part of the matrix; every stripe holds its 8 diagonal blocks, and the busiest stripe fills all 136 slots. `block_rows`: block row of a slot inside its stripe. `block_cols`: every slot's block column lies within 8 blocks of its global block row, counted around the loop of 1024 block columns; the live slots of a stripe name distinct blocks. `block_values`: the matrix assembled from the live slots is symmetric: live block (r, c) is the transpose of live block (c, r).
All inputs are finite; a program needn't handle non-finite values.
Results may differ from a plain program's by a relative error of at most 0.002.
The roundings to bfloat16 on the way count: a program that leaves them out, or rounds other values in their place, can miss the bound.
Values may be sent and summed in bfloat16 or wider, within the bound.
No kernel may reach another device: no remote copies, remote signals or barrier semaphores. Data moves between devices by JAX's collectives and lax.ppermute only.
A program may use at most 64 MiB of HBM per device.

v0:
```python
import math
import jax
import jax.numpy as jnp
from jax import lax
from jax.sharding import PartitionSpec as P


def extended_2(cells, sides, width):
    for axis, dim in sides:
        count = lax.axis_size(axis)
        head = lax.slice_in_dim(cells, 0, width, axis=dim)
        tail = lax.slice_in_dim(cells, cells.shape[dim] - width, cells.shape[dim], axis=dim)
        cells = jnp.concatenate(
            [
                lax.ppermute(tail, axis, [(i, (i + 1) % count) for i in range(count)]),
                cells,
                lax.ppermute(head, axis, [((i + 1) % count, i) for i in range(count)]),
            ],
            axis=dim,
        )
    return cells


def propagate(extended, block_values, local_index, placing, precise):
    channels = extended.shape[0]
    block_size = block_values.shape[1]
    blocked = extended.reshape(channels, extended.shape[1] // block_size, block_size)
    gathered = jnp.take(blocked, local_index, axis=1)
    if precise:
        products = jnp.einsum(
            "csb,sab->csa",
            gathered,
            block_values.astype(jnp.float32),
            precision=lax.Precision.HIGHEST,
        )
    else:
        products = jnp.einsum(
            "csb,sab->csa", gathered, block_values, preferred_element_type=jnp.float32
        )
    placed = jnp.einsum("csa,sr->cra", products, placing, precision=lax.Precision.HIGHEST)
    return placed.reshape(channels, placing.shape[1] * block_size)


def activation(entry_value):
    return jax.nn.gelu(entry_value, approximate=True)


def on_device(
    features, block_values, block_rows, block_cols, block_count, labels, weight_in, weight_out
):
    device_count = lax.axis_size("blk")
    stripe_index = lax.axis_index("blk")
    block_size = block_values.shape[1]
    slot_count = block_rows.shape[0]
    stripe_rows = features.shape[1]
    stripe_blocks = stripe_rows // block_size
    reach_blocks = (slot_count // stripe_blocks - 1) // 2
    total_blocks = stripe_blocks * device_count
    local_index = jnp.mod(block_cols - (stripe_index * stripe_blocks - reach_blocks), total_blocks)
    live_slots = jnp.arange(slot_count, dtype=jnp.int32) < block_count[0]
    placing = (
        (block_rows[:, None] == jnp.arange(stripe_blocks, dtype=jnp.int32)[None, :])
        & live_slots[:, None]
    ).astype(jnp.float32)
    band_width = reach_blocks * block_size
    node_scale = 1.0 / math.sqrt(device_count * stripe_rows)
    input_ext = extended_2(features, (("blk", 1),), band_width)
    prop_in = propagate(input_ext, block_values, local_index, placing, False).astype(jnp.bfloat16)
    prop_rows_in = lax.all_to_all(prop_in, "feat", split_axis=1, concat_axis=0, tiled=True)
    pre_hidden = jnp.einsum(
        "ih,ir->hr", weight_in, prop_rows_in, preferred_element_type=jnp.float32
    )
    hidden = activation(pre_hidden).astype(jnp.bfloat16)
    hidden_cols = lax.all_to_all(hidden, "feat", split_axis=0, concat_axis=1, tiled=True)
    hidden_ext = extended_2(hidden_cols, (("blk", 1),), band_width)
    prop_hid = propagate(hidden_ext, block_values, local_index, placing, False).astype(jnp.bfloat16)
    prop_rows_hid = lax.all_to_all(prop_hid, "feat", split_axis=1, concat_axis=0, tiled=True)
    logits = jnp.einsum("hc,hr->cr", weight_out, prop_rows_hid, preferred_element_type=jnp.float32)
    class_count = weight_out.shape[1]
    shifted = logits - jnp.max(logits, axis=0, keepdims=True)
    exponent = jnp.exp(shifted)
    probability = exponent / jnp.sum(exponent, axis=0, keepdims=True)
    onehot = (labels[None, :] == jnp.arange(class_count, dtype=jnp.int32)[:, None]).astype(
        jnp.float32
    )
    dlogits = ((probability - onehot) * node_scale).astype(jnp.bfloat16)
    out_share = jnp.einsum("hr,cr->hc", prop_rows_hid, dlogits, preferred_element_type=jnp.float32)
    grad_out = lax.psum(out_share, ("blk", "feat"))
    back_rows = jnp.einsum("hc,cr->hr", weight_out, dlogits, preferred_element_type=jnp.float32)
    back_cols = lax.all_to_all(
        back_rows.astype(jnp.bfloat16), "feat", split_axis=0, concat_axis=1, tiled=True
    ).astype(back_rows.dtype)
    back_ext = extended_2(back_cols.astype(jnp.bfloat16), (("blk", 1),), band_width).astype(
        back_cols.dtype
    )
    back_prop = propagate(back_ext, block_values, local_index, placing, True)
    back_hid = lax.all_to_all(
        back_prop.astype(jnp.bfloat16), "feat", split_axis=1, concat_axis=0, tiled=True
    ).astype(back_prop.dtype)
    unused_output, pullback = jax.vjp(activation, pre_hidden)
    grad_pre = pullback(back_hid)[0].astype(jnp.bfloat16)
    in_share = jnp.einsum("ir,hr->ih", prop_rows_in, grad_pre, preferred_element_type=jnp.float32)
    grad_in = lax.psum(in_share, ("blk", "feat"))
    return (logits, grad_in, grad_out)


def solution(mesh):
    placed = (
        P("feat", "blk"),
        P("blk", None, None),
        P("blk"),
        P("blk"),
        P("blk"),
        P(("blk", "feat")),
        P(),
        P(),
    )
    return jax.shard_map(
        on_device,
        mesh=mesh,
        in_specs=placed,
        out_specs=(P(None, ("blk", "feat")), P(), P()),
        check_vma=False,
    )
```

profile of v0, /device:TPU:2, one launch (start us, length us, event | category | flops | bytes accessed | tf_op | source)
XLA Modules:
  0.0 618.4 jit_solution(3650204196831870399)
XLA Ops:
  7.2 3.5 collective-permute-start
  10.7 6.3 %collective-permute-start.1 = (bf16[64,1024]{1,0:T(8,128)(2,1)}, bf16[64,1024]{1,0:T(8,128)(2,1)S(1)}, u32[]{:S(2)}, u32[]{:S(2)}) collective-permute-start(bf16[64,1024]{1,0:T(8,128)(2,1)} %param.10), channel_id=1, source_target_pairs={{4,0},{8,4},{12,8},{16,12},{20,16},{24,20},{28,24},{32,28},{36,32}... | collective-permute-start | bytes 393224 | tf_op jit(solution)/shard_map/ppermute | solution.py:17
  17.7 0.7 compare_and_fusion
  18.4 1.4 collective-permute-done.1
  19.9 1.0 copy_bitcast_fusion
  20.9 1.0 gather_fusion.1
  21.9 5.4 fusion.19
  27.3 4.0 fusion.43
  31.3 0.1 convert_element_type.67
  31.4 7.0 %all_to_all.80 = bf16[64,4,256]{2,0,1:T(8,128)(2,1)S(1)} all-to-all(bf16[64,4,256]{2,0,1:T(8,128)(2,1)S(1)} %copy.36), channel_id=1, replica_groups=mesh['blk'=128,'feat'=4] {'feat'}, dimensions={1} | all-to-all | bytes 262144 | tf_op jit(solution)/shard_map/all_to_all | solution.py:69
  38.4 0.3 multiply_convert_fusion
  38.7 7.0 %all_to_all.81 = bf16[4,64,256]{2,1,0:T(8,128)(2,1)S(1)} all-to-all(bf16[4,64,256]{2,1,0:T(8,128)(2,1)S(1)} %bitcast.120), channel_id=1, replica_groups=mesh['blk'=128,'feat'=4] {'feat'}, dimensions={0} | all-to-all | bytes 262144 | tf_op jit(solution)/shard_map/all_to_all | solution.py:74
  45.7 11.1 %collective-permute-start.3 = (bf16[64,1024]{1,0:T(8,128)(2,1)S(1)}, bf16[64,1024]{1,0:T(8,128)(2,1)S(1)}, u32[]{:S(2)}, u32[]{:S(2)}) collective-permute-start(bf16[64,1024]{1,0:T(8,128)(2,1)S(1)} %bitcast.116), channel_id=1, source_target_pairs={{4,0},{8,4},{12,8},{16,12},{20,16},{24,20},{28,24},{32,28},{36,32}... | collective-permute-start | bytes 393224 | tf_op jit(solution)/shard_map/ppermute | solution.py:17
  56.8 2.1 collective-permute-start.2
  58.9 0.1 copy.37
  59.0 0.1 concatenate.25
  59.1 0.2 collective-permute-done.3
  59.3 10.4 %collective-permute-done.2 = bf16[64,1024]{1,0:T(8,128)(2,1)S(1)} collective-permute-done((bf16[64,1024]{1,0:T(8,128)(2,1)S(1)}, bf16[64,1024]{1,0:T(8,128)(2,1)S(1)}, u32[]{:S(2)}, u32[]{:S(2)}) %collective-permute-start.2) | collective-permute-done | bytes 131104 | tf_op jit(solution)/shard_map/ppermute | solution.py:15
  69.8 1.0 gather_fusion.2
  70.8 5.4 fusion.22
  76.2 4.0 fusion.40
  80.3 0.1 convert_element_type.71
  80.4 7.0 %all_to_all.82 = bf16[64,4,256]{2,0,1:T(8,128)(2,1)S(1)} all-to-all(bf16[64,4,256]{2,0,1:T(8,128)(2,1)S(1)} %copy.43), channel_id=1, replica_groups=mesh['blk'=128,'feat'=4] {'feat'}, dimensions={1} | all-to-all | bytes 262144 | tf_op jit(solution)/shard_map/all_to_all | solution.py:77
  87.4 0.2 fusion.75
  87.7 0.2 convolution_convert_fusion
  87.9 7.0 %all_to_all.83 = bf16[4,64,256]{2,1,0:T(8,128)(2,1)S(1)} all-to-all(bf16[4,64,256]{2,1,0:T(8,128)(2,1)S(1)} %bitcast.121), channel_id=1, replica_groups=mesh['blk'=128,'feat'=4] {'feat'}, dimensions={0} | all-to-all | bytes 262144 | tf_op jit(solution)/shard_map/all_to_all | solution.py:90
  94.9 9.6 %collective-permute-start.5 = (bf16[64,1024]{1,0:T(8,128)(2,1)S(1)}, bf16[64,1024]{1,0:T(8,128)(2,1)S(1)}, u32[]{:S(2)}, u32[]{:S(2)}) collective-permute-start(bf16[64,1024]{1,0:T(8,128)(2,1)S(1)} %bitcast.118), channel_id=1, source_target_pairs={{4,0},{8,4},{12,8},{16,12},{20,16},{24,20},{28,24},{32,28},{36,32}... | collective-permute-start | bytes 393224 | tf_op jit(solution)/shard_map/ppermute | solution.py:17
  104.5 2.1 collective-permute-start.4
  106.7 0.1 copy.44
  106.8 0.1 concatenate.29
  106.9 0.1 collective-permute-done.5
  107.1 4.3 collective-permute-done.4
  111.4 0.1 maximum_convert_fusion
  111.5 2.9 gather_fusion
  114.4 11.1 %fusion.25 = f32[64,136,128]{2,0,1:T(8,128)S(1)} fusion(bf16[136,128,128]{2,1,0:T(8,128)(2,1)} %param.11, f32[136,64,128]{2,1,0:T(8,128)} %gather_fusion, pred[136]{0:T(512)(128)(4,1)S(1)} %get-tuple-element.6), kind=kOutput, calls=%fused_computation.24 | convolution fusion | flops 1712390144 | bytes 13369480 | tf_op jit(solution)/shard_map/csb,sab->csa/dot_general | solution.py:30
  125.4 4.0 fusion.37
  129.5 0.1 convert_element_type.79
  129.6 0.7 copy.50
  130.2 3.3 all-to-all-start.4
  133.6 0.0 all-reduce.3.cloned.1.call-start
  133.6 0.9 fusion.74
  134.5 3.7 all-to-all-done.4
  138.1 0.2 fusion.54
  138.3 0.9 fusion.76
  139.3 0.0 all-reduce.3.cloned.1.call-update
  139.3 469.0 %all-reduce.3.cloned.1.call-done = (f32[256,256]{1,0:T(8,128)}, f32[256,128]{1,0:T(8,128)}) async-done(((f32[256,256]{1,0:T(8,128)}, f32[256,128]{1,0:T(8,128)}), (f32[256,256]{1,0:T(8,128)}, f32[256,128]{1,0:T(8,128)})) %all-reduce.3.cloned.1.call-update) | async-done | bytes 393232 | tf_op jit(solution)/shard_map/psum | solution.py:103
  608.3 1.7 copy.84
  610.0 1.6 copy.85
  (25 shorter events, 0.3 us)
Async XLA Ops:
  7.2 31.2 %copy-start = (bf16[256,256]{1,0:T(8,128)(2,1)S(1)}, bf16[256,256]{1,0:T(8,128)(2,1)}, u32[]{:S(2)}) copy-start(bf16[256,256]{1,0:T(8,128)(2,1)} %param.16) | copy-start | bytes 393220
  7.2 11.2 %collective-permute-start = (bf16[64,1024]{1,0:T(8,128)(2,1)}, bf16[64,1024]{1,0:T(8,128)(2,1)S(1)}, u32[]{:S(2)}, u32[]{:S(2)}) collective-permute-start(bf16[64,1024]{1,0:T(8,128)(2,1)} %param.10), channel_id=1, source_target_pairs={{0,4},{4,8},{8,12},{12,16},{16,20},{20,24},{24,28},{28,32},{32,36}... | collective-permute-start | bytes 393224 | tf_op jit(solution)/shard_map/ppermute | solution.py:15
  10.7 9.1 %collective-permute-start.1 = (bf16[64,1024]{1,0:T(8,128)(2,1)}, bf16[64,1024]{1,0:T(8,128)(2,1)S(1)}, u32[]{:S(2)}, u32[]{:S(2)}) collective-permute-start(bf16[64,1024]{1,0:T(8,128)(2,1)} %param.10), channel_id=1, source_target_pairs={{4,0},{8,4},{12,8},{16,12},{20,16},{24,20},{28,24},{32,28},{36,32}... | collective-permute-start | bytes 393224 | tf_op jit(solution)/shard_map/ppermute | solution.py:17
  21.9 5.4 copy-start.3
  45.7 13.6 %collective-permute-start.3 = (bf16[64,1024]{1,0:T(8,128)(2,1)S(1)}, bf16[64,1024]{1,0:T(8,128)(2,1)S(1)}, u32[]{:S(2)}, u32[]{:S(2)}) collective-permute-start(bf16[64,1024]{1,0:T(8,128)(2,1)S(1)} %bitcast.116), channel_id=1, source_target_pairs={{4,0},{8,4},{12,8},{16,12},{20,16},{24,20},{28,24},{32,28},{36,32}... | collective-permute-start | bytes 393224 | tf_op jit(solution)/shard_map/ppermute | solution.py:17
  56.8 12.9 %collective-permute-start.2 = (bf16[64,1024]{1,0:T(8,128)(2,1)S(1)}, bf16[64,1024]{1,0:T(8,128)(2,1)S(1)}, u32[]{:S(2)}, u32[]{:S(2)}) collective-permute-start(bf16[64,1024]{1,0:T(8,128)(2,1)S(1)} %bitcast.117), channel_id=1, source_target_pairs={{0,4},{4,8},{8,12},{12,16},{16,20},{20,24},{24,28},{28,32},{32,36}... | collective-permute-start | bytes 393224 | tf_op jit(solution)/shard_map/ppermute | solution.py:15
  76.2 11.2 %copy-start.2 = (bf16[256,128]{1,0:T(8,128)(2,1)S(1)}, bf16[256,128]{1,0:T(8,128)(2,1)}, u32[]{:S(2)}) copy-start(bf16[256,128]{1,0:T(8,128)(2,1)} %param.17) | copy-start | bytes 196612
  76.2 11.5 %copy-start.4 = (s32[256]{0:T(256)S(1)}, s32[256]{0:T(256)}, u32[]{:S(2)}) copy-start(s32[256]{0:T(256)} %param.15) | copy-start | bytes 3076
  87.6 46.0 %copy-start.1 = (f32[256,128]{0,1:T(8,128)}, f32[256,128]{0,1:T(8,128)S(1)}, u32[]{:S(2)}) copy-start(f32[256,128]{0,1:T(8,128)S(1)} %get-tuple-element.11) | copy-start | bytes 393220
  94.9 12.2 %collective-permute-start.5 = (bf16[64,1024]{1,0:T(8,128)(2,1)S(1)}, bf16[64,1024]{1,0:T(8,128)(2,1)S(1)}, u32[]{:S(2)}, u32[]{:S(2)}) collective-permute-start(bf16[64,1024]{1,0:T(8,128)(2,1)S(1)} %bitcast.118), channel_id=1, source_target_pairs={{4,0},{8,4},{12,8},{16,12},{20,16},{24,20},{28,24},{32,28},{36,32}... | collective-permute-start | bytes 393224 | tf_op jit(solution)/shard_map/ppermute | solution.py:17
  104.5 6.9 %collective-permute-start.4 = (bf16[64,1024]{1,0:T(8,128)(2,1)S(1)}, bf16[64,1024]{1,0:T(8,128)(2,1)S(1)}, u32[]{:S(2)}, u32[]{:S(2)}) collective-permute-start(bf16[64,1024]{1,0:T(8,128)(2,1)S(1)} %bitcast.119), channel_id=1, source_target_pairs={{0,4},{4,8},{8,12},{12,16},{16,20},{20,24},{24,28},{28,32},{32,36}... | collective-permute-start | bytes 393224 | tf_op jit(solution)/shard_map/ppermute | solution.py:15
  130.2 7.9 %all-to-all-start.4 = ((bf16[64,4,256]{2,0,1:T(8,128)(2,1)}), bf16[64,4,256]{2,0,1:T(8,128)(2,1)S(1)}, u32[]{:S(2)}, u32[]{:S(2)}) async-start(bf16[64,4,256]{2,0,1:T(8,128)(2,1)} %copy.50), calls=%async_computation.4 | async-start | bytes 262144 | tf_op jit(solution)/shard_map/all_to_all | solution.py:97
  133.6 474.8 %all-reduce.3.cloned.1.call-start = ((), (), s32[]{:S(2)}) async-start(), calls=%async_computation.5 | async-start | bytes 786432 | tf_op jit(solution)/shard_map/psum | solution.py:103
Sparse Core Ops, SparseCore 0:
  140.4 467.8 all-reduce.2
where the time goes:
time: 619 us; the launch traced here: 618 us
  waiting for transfers between devices  489 us (79%)
  starting transfers between devices  38.2 us (6%)
  matrix products  36.4 us (6%)
  blocking collectives  28 us (5%)
  between operations  15 us (2%)
  local copies, waits for them, and re-layouts  9.57 us (2%)
    psum x1, waiting for transfers between devices, on_device(): grad_in = lax.psum(in_share, ('blk', 'feat'))  469 us
    ppermute x3, starting transfers between devices, extended_2(): lax.ppermute(head, axis, [((i + 1) % count, i) for i in range(count)])  27.1 us
    ppermute x3, waiting for transfers between devices, extended_2(): lax.ppermute(tail, axis, [(i, (i + 1) % count) for i in range(count)])  14.8 us
  transfers between devices with their start and end apart: 8, of which 7 were waited for; matrix products, arithmetic and copies ran while one was open for 0% of the time, Pallas kernels for 0%

commit v1 on v0

--- a/solution.py
+++ b/solution.py
@@ -100,7 +100,9 @@
     unused_output, pullback = jax.vjp(activation, pre_hidden)
     grad_pre = pullback(back_hid)[0].astype(jnp.bfloat16)
     in_share = jnp.einsum("ir,hr->ih", prop_rows_in, grad_pre, preferred_element_type=jnp.float32)
-    grad_in = lax.psum(in_share, ("blk", "feat"))
+    grad_in = in_share
+    for mesh_axis in ("blk", "feat"):
+        grad_in = lax.psum(grad_in, mesh_axis)
     return (logits, grad_in, grad_out)
 
 

time: 619 us -> 1870 us (3.02)
  the two profiles are of different devices: /device:TPU:2 before, /device:TPU:1 now
where the time goes in v1:
time: 1870 us
  waiting for transfers between devices  1730 us (93%)
  blocking collectives  38 us (2%)
  matrix products  36.4 us (2%)
  starting transfers between devices  36.1 us (2%)
    psum x2, waiting for transfers between devices, on_device(): grad_in = lax.psum(grad_in, mesh_axis)  1220 us
    psum x1, waiting for transfers between devices, on_device(): grad_out = lax.psum(out_share, ('blk', 'feat'))  491 us
  transfers between devices with their start and end apart: 9, of which 7 were waited for; matrix products, arithmetic and copies ran while one was open for 0% of the time, Pallas kernels for 0%

profile of v1, /device:TPU:1, one launch (start us, length us, event | category | flops | bytes accessed | tf_op | source)
XLA Modules:
  0.0 1866.4 jit_solution(16552248980187968288)
XLA Ops:
  7.2 0.0 all-reduce.4.cloned.1.call-start
  7.2 3.9 collective-permute-start
  11.2 14.8 collective-permute-start.1
  26.6 0.7 compare_and_fusion
  27.3 0.1 collective-permute-done
  27.4 1.0 collective-permute-done.1
  28.4 1.0 copy_bitcast_fusion
  29.4 1.0 gather_fusion.1
  30.4 5.4 fusion.19
  35.8 4.0 fusion.43
  39.8 0.1 convert_element_type.67
  40.0 7.5 all_to_all.80
  47.4 0.3 multiply_convert_fusion
  47.7 7.0 all_to_all.81
  54.7 9.7 collective-permute-start.3
  64.5 2.1 collective-permute-start.2
  66.6 0.1 copy.37
  66.7 0.1 concatenate.25
  66.8 9.1 collective-permute-done.2
  76.0 1.0 gather_fusion.2
  77.0 5.4 fusion.22
  82.4 4.0 fusion.40
  86.4 0.1 convert_element_type.71
  86.5 8.4 all_to_all.82
  94.9 0.2 fusion.75
  95.2 0.2 convolution_convert_fusion
  95.4 7.0 all_to_all.83
  102.4 1.9 collective-permute-start.5
  104.4 3.6 collective-permute-start.4
  108.0 0.1 copy.44
  108.1 0.1 concatenate.29
  108.2 7.6 collective-permute-done.4
  115.8 0.1 maximum_convert_fusion
  115.9 2.9 gather_fusion
  118.8 11.1 fusion.25
  129.9 4.0 fusion.37
  133.9 0.1 convert_element_type.79
  134.0 8.1 all_to_all.84
  142.1 0.2 fusion.54
  142.3 0.9 fusion.76
  143.3 0.0 all-reduce.8.cloned.1.call-start
  143.4 0.9 fusion.74
  144.2 0.0 all-reduce.6.cloned.1.call-start
  144.3 1175.7 %all-reduce.4.cloned.1.call-done = f32[256,256]{1,0:T(8,128)} async-done(((f32[256,256]{1,0:T(8,128)}), f32[256,256]{1,0:T(8,128)}) %all-reduce.4.cloned.1.call-update) | async-done | bytes 262160 | tf_op jit(solution)/shard_map/psum | solution.py:105
  1320.1 491.3 %all-reduce.8.cloned.1.call-done = f32[256,128]{1,0:T(8,128)} async-done(((f32[256,128]{1,0:T(8,128)}), f32[256,128]{1,0:T(8,128)}) %all-reduce.8.cloned.1.call-update) | async-done | bytes 131088 | tf_op jit(solution)/shard_map/psum | solution.py:88
  1811.4 45.2 %all-reduce.6.cloned.1.call-done = f32[256,256]{1,0:T(8,128)} async-done(((f32[256,256]{1,0:T(8,128)}), f32[256,256]{1,0:T(8,128)}) %all-reduce.6.cloned.1.call-update) | async-done | bytes 262160 | tf_op jit(solution)/shard_map/psum | solution.py:105
  1856.6 1.7 copy.85
  1858.3 1.6 copy.86
  (30 shorter events, 0.4 us)
Async XLA Ops:
  7.2 40.3 %copy-start = (bf16[256,256]{1,0:T(8,128)(2,1)S(1)}, bf16[256,256]{1,0:T(8,128)(2,1)}, u32[]{:S(2)}) copy-start(bf16[256,256]{1,0:T(8,128)(2,1)} %param.16) | copy-start | bytes 393220
  7.2 1312.9 %all-reduce.4.cloned.1.call-start = ((), (), s32[]{:S(2)}) async-start(), calls=%async_computation.5 | async-start | bytes 524288 | tf_op jit(solution)/shard_map/psum | solution.py:105
  7.2 20.2 %collective-permute-start = (bf16[64,1024]{1,0:T(8,128)(2,1)}, bf16[64,1024]{1,0:T(8,128)(2,1)S(1)}, u32[]{:S(2)}, u32[]{:S(2)}) collective-permute-start(bf16[64,1024]{1,0:T(8,128)(2,1)} %param.10), channel_id=1, source_target_pairs={{0,4},{4,8},{8,12},{12,16},{16,20},{20,24},{24,28},{28,32},{32,36}... | collective-permute-start | bytes 393224 | tf_op jit(solution)/shard_map/ppermute | solution.py:15
  11.2 17.2 collective-permute-start.1
  30.4 5.4 copy-start.3
  54.7 12.1 collective-permute-start.3
  64.5 11.4 collective-permute-start.2
  82.3 12.6 copy-start.2
  82.4 12.9 copy-start.4
  95.2 48.2 %copy-start.1 = (f32[256,128]{0,1:T(8,128)}, f32[256,128]{0,1:T(8,128)S(1)}, u32[]{:S(2)}) copy-start(f32[256,128]{0,1:T(8,128)S(1)} %get-tuple-element.9) | copy-start | bytes 393220
  102.4 5.7 collective-permute-start.5
  104.4 11.4 collective-permute-start.4
  143.3 1668.1 %all-reduce.8.cloned.1.call-start = ((), (), s32[]{:S(2)}) async-start(), calls=%async_computation.7 | async-start | bytes 262144 | tf_op jit(solution)/shard_map/psum | solution.py:88
  144.2 1712.4 %all-reduce.6.cloned.1.call-start = ((), (), s32[]{:S(2)}) async-start(), calls=%async_computation.6 | async-start | bytes 524288 | tf_op jit(solution)/shard_map/psum | solution.py:105
Sparse Core Ops, SparseCore 0:
  143.4 1176.5 all-reduce.3
  1326.1 485.2 all-reduce.7
  1814.3 42.2 all-reduce.5
